TPU v7x, 256 devices: a whole 4x4x8 slice. The times are simulated.
256 devices in a mesh: gx: 16 (over y, x_hi, core), gy: 16 (over x_lo, z).
Axes of the slice: x: 4 (x_hi: 2, x_lo: 2; x = x_hi * 2 + x_lo), y: 4, z: 8, core: 2. Of those that a mesh axis runs over, the one named last changes fastest.
Arguments:
- source: bfloat16 [64, 32, 128, 128], P(None, 'gx', 'gy'), may hold values from -6 to 6
- preact: bfloat16 [64, 32, 128, 128], P(None, 'gx', 'gy'), may hold values from -6 to 6
- cotangent: bfloat16 [64, 32, 128, 128], P(None, 'gx', 'gy'), may hold values from -6 to 6
- kernel: bfloat16 [27, 64, 64], replicated, may hold values from -0.15625 to 0.15625
Outputs:
- grad_source: bfloat16 [64, 32, 128, 128], P(None, 'gx', 'gy')
- grad_kernel: float32 [110592], P(('gx', 'gy'))
All inputs are finite; a program needn't handle non-finite values.
Results may differ from a plain program's by a relative error of at most 0.007.
Values may be sent and summed in bfloat16 or wider, within the bound.
A program may use at most 64 MiB of HBM per device.

v0:
```python
import math

import jax
import jax.numpy as jnp
from jax import lax
from jax.sharding import PartitionSpec as P


def with_halo(cells, sides, width):
    for axis, dim in sides:
        count = lax.axis_size(axis)
        head = lax.slice_in_dim(cells, 0, width, axis=dim)
        tail = lax.slice_in_dim(cells, cells.shape[dim] - width, cells.shape[dim], axis=dim)
        cells = jnp.concatenate(
            [
                lax.ppermute(tail, axis, [(i, (i + 1) % count) for i in range(count)]),
                cells,
                lax.ppermute(head, axis, [((i + 1) % count, i) for i in range(count)]),
            ],
            axis=dim,
        )
    return cells


def on_device(source, preact, cotangent, kernel):
    channels, width_x, width_y, depth_cells = source.shape
    cell_count = width_x * width_y * depth_cells
    slope_grad = jnp.where(preact > 0, cotangent, jnp.zeros_like(cotangent))
    wide_slope = with_halo(slope_grad, (("gx", 1), ("gy", 2)), 1)
    wide_src = with_halo(source, (("gx", 1), ("gy", 2)), 1)
    slope_flat = slope_grad.reshape(channels, cell_count)
    kernel_grid = kernel.reshape(3, 3, 3, channels, channels)
    accumulated = jnp.zeros((channels, cell_count), jnp.float32)
    planes = []
    for c in range(3):
        shifted_slope = jnp.roll(wide_slope, c - 1, axis=3)
        slope_columns = jnp.stack(
            [
                shifted_slope[:, 2 - a : 2 - a + width_x, 2 - b : 2 - b + width_y, :]
                for a in range(3)
                for b in range(3)
            ],
            axis=0,
        )
        slope_columns = slope_columns.reshape(9 * channels, cell_count)
        shifted_src = jnp.roll(wide_src, 1 - c, axis=3)
        src_columns = jnp.stack(
            [
                shifted_src[:, a : a + width_x, b : b + width_y, :]
                for a in range(3)
                for b in range(3)
            ],
            axis=0,
        )
        src_columns = src_columns.reshape(9 * channels, cell_count)
        plane_grad = lax.dot_general(
            slope_flat, src_columns, (((1,), (1,)), ((), ())), preferred_element_type=jnp.float32
        )
        planes.append(plane_grad.reshape(channels, 3, 3, channels).transpose(1, 2, 0, 3))
        kernel_plane = kernel_grid[:, :, c].transpose(3, 0, 1, 2).reshape(channels, 9 * channels)
        accumulated = accumulated + jnp.dot(
            kernel_plane, slope_columns, preferred_element_type=jnp.float32
        )
    total_cells = cell_count * lax.axis_size("gx") * lax.axis_size("gy")
    norm_scale = 1.0 / math.sqrt(total_cells)
    kernel_term = jnp.stack(planes, axis=2).reshape(-1) * norm_scale
    grad_kernel = lax.psum_scatter(kernel_term, ("gx", "gy"), scatter_dimension=0, tiled=True)
    grad_source = accumulated.reshape(source.shape).astype(jnp.bfloat16)
    return (grad_source, grad_kernel)


def solution(mesh):
    placed = (P(None, "gx", "gy", None), P(None, "gx", "gy", None), P(None, "gx", "gy", None), P())
    return jax.shard_map(
        on_device,
        mesh=mesh,
        in_specs=placed,
        out_specs=(P(None, "gx", "gy", None), P(("gx", "gy"))),
        check_vma=False,
    )
```

profile of v0, /device:TPU:1, one launch (start us, length us, event | category | flops | bytes accessed | tf_op | source)
XLA Modules:
  0.0 338.0 jit_solution(7222421958731389059)
XLA Ops:
  7.2 1.1 fusion.75
  8.3 4.2 %collective-permute-start.4 = (bf16[64,1,8,128]{3,2,1,0:T(8,128)(2,1)S(1)}, bf16[64,1,8,128]{3,2,1,0:T(8,128)(2,1)S(1)}, u32[]{:S(2)}, u32[]{:S(2)}) collective-permute-start(bf16[64,1,8,128]{3,2,1,0:T(8,128)(2,1)S(1)} %get-tuple-element.18), channel_id=1, source_target_pairs={{0,16},{16,32},{32,48},{48,64},{64,80},{80,96},{96,112},{112,128},... | collective-permute-start | bytes 393224 | tf_op jit(solution)/shard_map/ppermute | solution.py:16
  12.5 1.1 compare_select_fusion
  13.6 3.3 collective-permute-start
  16.9 1.3 collective-permute-start.1
  20.6 4.5 %collective-permute-start.7 = (bf16[64,4,1,128]{3,2,1,0:T(2,128)(2,1)S(1)}, bf16[64,4,1,128]{3,2,1,0:T(2,128)(2,1)S(1)}, u32[]{:S(2)}, u32[]{:S(2)}) collective-permute-start(bf16[64,4,1,128]{3,2,1,0:T(2,128)(2,1)S(1)} %get-tuple-element.11), channel_id=1, source_target_pairs={{1,0},{2,1},{3,2},{4,3},{5,4},{6,5},{7,6},{8,7},{9,8},{10,9},{11,1... | collective-permute-start | bytes 196616 | tf_op jit(solution)/shard_map/ppermute | solution.py:18
  25.4 4.8 %collective-permute-start.3 = (bf16[64,4,1,128]{3,2,1,0:T(2,128)(2,1)S(1)}, bf16[64,4,1,128]{3,2,1,0:T(2,128)(2,1)S(1)}, u32[]{:S(2)}, u32[]{:S(2)}) collective-permute-start(bf16[64,4,1,128]{3,2,1,0:T(2,128)(2,1)S(1)} %get-tuple-element.13), channel_id=1, source_target_pairs={{1,0},{2,1},{3,2},{4,3},{5,4},{6,5},{7,6},{8,7},{9,8},{10,9},{11,1... | collective-permute-start | bytes 196616 | tf_op jit(solution)/shard_map/ppermute | solution.py:18
  34.7 1.6 fusion.72
  42.1 1.4 copy-done.10
  43.5 1.4 copy-done.11
  44.9 5.0 %dot_general.27 = bf16[3,3,64,2048]{3,2,1,0:T(8,128)(2,1)} reshape(bf16[9,64,2,8,128]{4,3,2,1,0:T(8,128)(2,1)} %copy-done.10) | data formatting | bytes 4718592 | tf_op jit(solution)/shard_map/dot_general | solution.py:56
  49.9 4.9 %dot_general.31 = bf16[3,3,64,2048]{3,2,1,0:T(8,128)(2,1)} reshape(bf16[9,64,2,8,128]{4,3,2,1,0:T(8,128)(2,1)} %copy-done.11) | data formatting | bytes 4718592 | tf_op jit(solution)/shard_map/dot_general | solution.py:56
  54.8 3.8 %convolution_bitcast_fusion.2 = f32[3,3,1,64,64]{4,3,1,0,2:T(8,128)} fusion(bf16[3,3,64,2048]{3,2,1,0:T(8,128)(2,1)} %dot_general.27, bf16[64,2048,1,1]{1,0,2,3:T(8,128)(2,1)} %reshape.53), kind=kOutput, calls=%fused_computation.5 | convolution fusion | flops 150994944 | bytes 2768896 | tf_op jit(solution)/shard_map/dot_general | solution.py:56
  58.6 2.9 convolution_bitcast_fusion
  63.1 0.9 fusion.20
  68.0 0.9 fusion.13
  68.8 4.9 %dot_general.29 = bf16[3,3,64,2048]{3,2,1,0:T(8,128)(2,1)} reshape(bf16[9,64,2,8,128]{4,3,2,1,0:T(8,128)(2,1)} %fusion.13) | data formatting | bytes 4718592 | tf_op jit(solution)/shard_map/dot_general | solution.py:56
  73.8 3.0 convolution_bitcast_fusion.1
  76.9 1.0 copy.7
  77.9 2.2 mul.11
  80.2 1.5 fusion.65
  86.9 1.4 copy-done.12
  88.4 1.4 copy-done.13
  89.8 3.7 %reshape.45 = bf16[576,2048]{1,0:T(8,128)(2,1)S(1)} reshape(bf16[9,64,2,8,128]{4,3,2,1,0:T(8,128)(2,1)} %copy-done.12) | data formatting | bytes 4718592 | tf_op jit(solution)/shard_map/reshape | solution.py:45
  93.5 0.9 fusion.55
  98.4 0.9 fusion.49
  100.8 4.9 %reshape.48 = bf16[576,2048]{1,0:T(8,128)(2,1)} reshape(bf16[9,64,2,8,128]{4,3,2,1,0:T(8,128)(2,1)} %fusion.45) | data formatting | bytes 4718592 | tf_op jit(solution)/shard_map/reshape | solution.py:45
  105.8 5.0 %reshape.50 = bf16[576,2048]{1,0:T(8,128)(2,1)} reshape(bf16[9,64,2,8,128]{4,3,2,1,0:T(8,128)(2,1)} %copy-done.13) | data formatting | bytes 4718592 | tf_op jit(solution)/shard_map/reshape | solution.py:45
  111.4 1.1 copy-done.4
  113.1 1.1 copy-done.3
  115.5 214.3 %all-reduce.3.cloned.1.call-done = f32[110592]{0:T(1024)} async-done(((f32[110592]{0:T(1024)}), f32[110592]{0:T(1024)}) %all-reduce.3.cloned.1.call-update) | async-done | bytes 442384
  329.8 1.3 dynamic-slice
  (136 shorter events, 31.9 us)
Async XLA Ops:
  7.2 12.7 %copy-start.8 = (bf16[64,2,8,128]{3,2,1,0:T(8,128)(2,1)S(1)}, bf16[64,2,8,128]{3,2,1,0:T(8,128)(2,1)}, u32[]{:S(2)}) copy-start(bf16[64,2,8,128]{3,2,1,0:T(8,128)(2,1)} %param.4) | copy-start | bytes 786436
  7.2 11.9 %copy-start.31 = (bf16[27,64,64]{2,1,0:T(8,128)(2,1)S(1)}, bf16[27,64,64]{2,1,0:T(8,128)(2,1)}, u32[]{:S(2)}) copy-start(bf16[27,64,64]{2,1,0:T(8,128)(2,1)} %param.7) | copy-start | bytes 663556
  7.2 322.6 %all-reduce.3.cloned.1.call-start = ((), (), s32[]{:S(2)}) async-start(), calls=%async_computation | async-start | bytes 884736
  8.3 11.5 %collective-permute-start.4 = (bf16[64,1,8,128]{3,2,1,0:T(8,128)(2,1)S(1)}, bf16[64,1,8,128]{3,2,1,0:T(8,128)(2,1)S(1)}, u32[]{:S(2)}, u32[]{:S(2)}) collective-permute-start(bf16[64,1,8,128]{3,2,1,0:T(8,128)(2,1)S(1)} %get-tuple-element.18), channel_id=1, source_target_pairs={{0,16},{16,32},{32,48},{48,64},{64,80},{80,96},{96,112},{112,128},... | collective-permute-start | bytes 393224 | tf_op jit(solution)/shard_map/ppermute | solution.py:16
  12.5 7.4 %collective-permute-start.5 = (bf16[64,1,8,128]{3,2,1,0:T(8,128)(2,1)S(1)}, bf16[64,1,8,128]{3,2,1,0:T(8,128)(2,1)S(1)}, u32[]{:S(2)}, u32[]{:S(2)}) collective-permute-start(bf16[64,1,8,128]{3,2,1,0:T(8,128)(2,1)S(1)} %get-tuple-element.17), channel_id=1, source_target_pairs={{16,0},{32,16},{48,32},{64,48},{80,64},{96,80},{112,96},{128,112},... | collective-permute-start | bytes 393224 | tf_op jit(solution)/shard_map/ppermute | solution.py:18
  13.6 11.5 %collective-permute-start = (bf16[64,1,8,128]{3,2,1,0:T(8,128)(2,1)S(1)}, bf16[64,1,8,128]{3,2,1,0:T(8,128)(2,1)S(1)}, u32[]{:S(2)}, u32[]{:S(2)}) collective-permute-start(bf16[64,1,8,128]{3,2,1,0:T(8,128)(2,1)S(1)} %get-tuple-element.19), channel_id=1, source_target_pairs={{0,16},{16,32},{32,48},{48,64},{64,80},{80,96},{96,112},{112,128},... | collective-permute-start | bytes 393224 | tf_op jit(solution)/shard_map/ppermute | solution.py:16
  16.9 8.2 %collective-permute-start.1 = (bf16[64,1,8,128]{3,2,1,0:T(8,128)(2,1)S(1)}, bf16[64,1,8,128]{3,2,1,0:T(8,128)(2,1)S(1)}, u32[]{:S(2)}, u32[]{:S(2)}) collective-permute-start(bf16[64,1,8,128]{3,2,1,0:T(8,128)(2,1)S(1)} %get-tuple-element.20), channel_id=1, source_target_pairs={{16,0},{32,16},{48,32},{64,48},{80,64},{96,80},{112,96},{128,112},... | collective-permute-start | bytes 393224 | tf_op jit(solution)/shard_map/ppermute | solution.py:18
  19.8 12.8 %copy-start.29 = (bf16[64,1,8,128]{3,2,1,0:T(8,128)(2,1)}, bf16[64,1,8,128]{3,2,1,0:T(8,128)(2,1)S(1)}, u32[]{:S(2)}) copy-start(bf16[64,1,8,128]{3,2,1,0:T(8,128)(2,1)S(1)} %collective-permute-done.4) | copy-start | bytes 393220
  19.9 12.7 %copy-start.27 = (bf16[64,1,8,128]{3,2,1,0:T(8,128)(2,1)}, bf16[64,1,8,128]{3,2,1,0:T(8,128)(2,1)S(1)}, u32[]{:S(2)}) copy-start(bf16[64,1,8,128]{3,2,1,0:T(8,128)(2,1)S(1)} %collective-permute-done.5) | copy-start | bytes 393220
  20.0 10.2 %copy-start.1 = (bf16[64,4,8,128]{3,2,1,0:T(8,128)(2,1)}, bf16[64,4,8,128]{3,2,1,0:T(8,128)(2,1)S(1)}, u32[]{:S(2)}) copy-start(bf16[64,4,8,128]{3,2,1,0:T(8,128)(2,1)S(1)} %constant_dynamic-update-slice_fusion) | copy-start | bytes 1572868
  20.2 10.0 %collective-permute-start.6 = (bf16[64,4,1,128]{3,2,1,0:T(2,128)(2,1)S(1)}, bf16[64,4,1,128]{3,2,1,0:T(2,128)(2,1)S(1)}, u32[]{:S(2)}, u32[]{:S(2)}) collective-permute-start(bf16[64,4,1,128]{3,2,1,0:T(2,128)(2,1)S(1)} %get-tuple-element.10), channel_id=1, source_target_pairs={{0,1},{1,2},{2,3},{3,4},{4,5},{5,6},{6,7},{7,8},{8,9},{9,10},{10,1... | collective-permute-start | bytes 196616 | tf_op jit(solution)/shard_map/ppermute | solution.py:16
  20.6 9.6 %collective-permute-start.7 = (bf16[64,4,1,128]{3,2,1,0:T(2,128)(2,1)S(1)}, bf16[64,4,1,128]{3,2,1,0:T(2,128)(2,1)S(1)}, u32[]{:S(2)}, u32[]{:S(2)}) collective-permute-start(bf16[64,4,1,128]{3,2,1,0:T(2,128)(2,1)S(1)} %get-tuple-element.11), channel_id=1, source_target_pairs={{1,0},{2,1},{3,2},{4,3},{5,4},{6,5},{7,6},{8,7},{9,8},{10,9},{11,1... | collective-permute-start | bytes 196616 | tf_op jit(solution)/shard_map/ppermute | solution.py:18
  25.1 8.3 %copy-start.5 = (bf16[64,1,8,128]{3,2,1,0:T(8,128)(2,1)}, bf16[64,1,8,128]{3,2,1,0:T(8,128)(2,1)S(1)}, u32[]{:S(2)}) copy-start(bf16[64,1,8,128]{3,2,1,0:T(8,128)(2,1)S(1)} %collective-permute-done.1) | copy-start | bytes 393220
  25.3 8.1 %collective-permute-start.2 = (bf16[64,4,1,128]{3,2,1,0:T(2,128)(2,1)S(1)}, bf16[64,4,1,128]{3,2,1,0:T(2,128)(2,1)S(1)}, u32[]{:S(2)}, u32[]{:S(2)}) collective-permute-start(bf16[64,4,1,128]{3,2,1,0:T(2,128)(2,1)S(1)} %get-tuple-element.12), channel_id=1, source_target_pairs={{0,1},{1,2},{2,3},{3,4},{4,5},{5,6},{6,7},{7,8},{8,9},{9,10},{10,1... | collective-permute-start | bytes 196616 | tf_op jit(solution)/shard_map/ppermute | solution.py:16
  25.4 8.0 %collective-permute-start.3 = (bf16[64,4,1,128]{3,2,1,0:T(2,128)(2,1)S(1)}, bf16[64,4,1,128]{3,2,1,0:T(2,128)(2,1)S(1)}, u32[]{:S(2)}, u32[]{:S(2)}) collective-permute-start(bf16[64,4,1,128]{3,2,1,0:T(2,128)(2,1)S(1)} %get-tuple-element.13), channel_id=1, source_target_pairs={{1,0},{2,1},{3,2},{4,3},{5,4},{6,5},{7,6},{8,7},{9,8},{10,9},{11,1... | collective-permute-start | bytes 196616 | tf_op jit(solution)/shard_map/ppermute | solution.py:18
  54.8 3.8 %copy-start.7 = (bf16[3,3,64,2048]{3,2,1,0:T(8,128)(2,1)S(1)}, bf16[3,3,64,2048]{3,2,1,0:T(8,128)(2,1)}, u32[]{:S(2)}) copy-start(bf16[3,3,64,2048]{3,2,1,0:T(8,128)(2,1)} %dot_general.31) | copy-start | bytes 7077892
  54.8 6.7 %copy-start.2 = (bf16[64,4,8,128]{3,2,1,0:T(8,128)(2,1)S(1)}, bf16[64,4,8,128]{3,2,1,0:T(8,128)(2,1)}, u32[]{:S(2)}) copy-start(bf16[64,4,8,128]{3,2,1,0:T(8,128)(2,1)} %copy-done.1) | copy-start | bytes 1572868
  54.8 6.7 %copy-start.21 = (bf16[64,4,1,128]{3,2,1,0:T(2,128)(2,1)S(1)}, bf16[64,4,1,128]{3,2,1,0:T(2,128)(2,1)}, u32[]{:S(2)}) copy-start(bf16[64,4,1,128]{3,2,1,0:T(2,128)(2,1)} %copy-done.20) | copy-start | bytes 196612
  58.6 3.8 %copy-start.9 = (bf16[64,2,8,128]{3,2,1,0:T(8,128)(2,1)S(1)}, bf16[64,2,8,128]{3,2,1,0:T(8,128)(2,1)}, u32[]{:S(2)}) copy-start(bf16[64,2,8,128]{3,2,1,0:T(8,128)(2,1)} %param.4) | copy-start | bytes 786436
  58.6 3.8 %copy-start.30 = (bf16[64,1,8,128]{3,2,1,0:T(8,128)(2,1)S(1)}, bf16[64,1,8,128]{3,2,1,0:T(8,128)(2,1)}, u32[]{:S(2)}) copy-start(bf16[64,1,8,128]{3,2,1,0:T(8,128)(2,1)} %copy-done.29) | copy-start | bytes 393220
  58.6 4.5 %copy-start.19 = (bf16[64,4,1,128]{3,2,1,0:T(2,128)(2,1)S(1)}, bf16[64,4,1,128]{3,2,1,0:T(2,128)(2,1)}, u32[]{:S(2)}) copy-start(bf16[64,4,1,128]{3,2,1,0:T(2,128)(2,1)} %copy-done.18) | copy-start | bytes 196612
  62.3 4.9 %copy-start.28 = (bf16[64,1,8,128]{3,2,1,0:T(8,128)(2,1)S(1)}, bf16[64,1,8,128]{3,2,1,0:T(8,128)(2,1)}, u32[]{:S(2)}) copy-start(bf16[64,1,8,128]{3,2,1,0:T(8,128)(2,1)} %copy-done.27) | copy-start | bytes 393220
  73.8 3.0 copy-start.22
  73.8 3.0 copy-start.23
  89.8 3.7 %copy-start.6 = (bf16[64,1,8,128]{3,2,1,0:T(8,128)(2,1)S(1)}, bf16[64,1,8,128]{3,2,1,0:T(8,128)(2,1)}, u32[]{:S(2)}) copy-start(bf16[64,1,8,128]{3,2,1,0:T(8,128)(2,1)} %copy-done.5) | copy-start | bytes 393220
  89.8 3.7 %copy-start.17 = (bf16[64,4,1,128]{3,2,1,0:T(2,128)(2,1)S(1)}, bf16[64,4,1,128]{3,2,1,0:T(2,128)(2,1)}, u32[]{:S(2)}) copy-start(bf16[64,4,1,128]{3,2,1,0:T(2,128)(2,1)} %copy-done.16) | copy-start | bytes 196612
  89.8 5.4 %copy-start.15 = (bf16[64,4,1,128]{3,2,1,0:T(2,128)(2,1)S(1)}, bf16[64,4,1,128]{3,2,1,0:T(2,128)(2,1)}, u32[]{:S(2)}) copy-start(bf16[64,4,1,128]{3,2,1,0:T(2,128)(2,1)} %copy-done.14) | copy-start | bytes 196612
  105.8 5.0 %copy-start.26 = (bf16[3,3,1,64,64]{4,3,2,1,0:T(8,128)(2,1)S(1)}, bf16[3,3,1,64,64]{4,3,2,1,0:T(8,128)(2,1)}, u32[]{:S(2)}) copy-start(bf16[3,3,1,64,64]{4,3,2,1,0:T(8,128)(2,1)} %get-tuple-element.16) | copy-start | bytes 221188
  110.8 1.7 copy-start.4
  110.8 1.7 copy-start.25
  112.4 1.7 copy-start.3
  112.4 1.7 copy-start.24
  (9 other events, 11.0 us)
Sparse Core Ops, SparseCore 0:
  80.3 249.5 all-reduce.2
where the time goes:
time: 339 us; the launch traced here: 338 us
  waiting for transfers between devices  215 us (63%)
  local copies, waits for them, and re-layouts  50.5 us (15%)
  other arithmetic  28.3 us (8%)
  starting transfers between devices  18.7 us (6%)
  between operations  14.5 us (4%)
  matrix products  11.5 us (3%)
    unnamed x2, waiting for transfers between devices  214 us
    unnamed x46, other arithmetic  22.7 us
    dot_general x3, local copies, waits for them, and re-layouts, on_device(): lax.dot_general(slope_flat, src_columns, (((1,), (1,)), ((), ())), prefer...  14.8 us
    reshape x3, local copies, waits for them, and re-layouts, on_device(): slope_columns = slope_columns.reshape(9 * channels, cell_count)  13.6 us
    unnamed x70, local copies, waits for them, and re-layouts  12.8 us
    ppermute x4, starting transfers between devices, with_halo(): lax.ppermute(head, axis, [((i + 1) % count, i) for i in range(count)])  10.6 us
    dot_general x3, matrix products, on_device(): lax.dot_general(slope_flat, src_columns, (((1,), (1,)), ((), ())), prefer...  9.67 us
    ppermute x4, starting transfers between devices, with_halo(): lax.ppermute(tail, axis, [(i, (i + 1) % count) for i in range(count)])  8.03 us
  transfers between devices with their start and end apart: 9, of which 2 were waited for; matrix products, arithmetic and copies ran while one was open for 10% of the time, Pallas kernels for 0%

commit v1 on v0

v1 whole, which is shorter than its diff:
```python
import math

import jax
import jax.numpy as jnp
from jax import lax
from jax.experimental import pallas as pl
from jax.experimental.pallas import tpu as pltpu
from jax.sharding import PartitionSpec as P

MESH = pl.DeviceIdType.MESH
F32, BF16 = jnp.float32, jnp.bfloat16
C, NZ = 64, 128
WX, WY = 2, 8
DEPTH = 8
ROWS = 27
OWN = 432
CELLS = 32 * 128 * 128
NT = (((1,), (1,)), ((), ()))


def spot(y, x, core, z):
    return (
        (y * 2 + lax.div(x, 2)) * 2 + core,
        lax.rem(x, 2) * DEPTH + z,
    )


def body(
    source, preact, cotangent, kernel, gs_out, gk_out,
    pv, cv, sv, kv, wide, wide_src, wide_out, slope, src3, weights, prod_lo, prod_hi,
    part, core_in, half, a_in, quarter, b_in, last, z_out, z_in,
    load_sem, halo_send, halo_recv, core_send, core_recv, a_send, a_recv, b_send, b_recv, z_send, z_recv,
):
    gx, gy = lax.axis_index("gx"), lax.axis_index("gy")
    core, xhi, y = lax.rem(gx, 2), lax.rem(lax.div(gx, 2), 2), lax.div(gx, 4)
    xlo, z = lax.div(gy, DEPTH), lax.rem(gy, DEPTH)
    x = xhi * 2 + xlo
    other = 1 - core

    up_x, dn_x = lax.rem(gx + 1, 16), lax.rem(gx + 15, 16)
    up_y, dn_y = lax.rem(gy + 1, 16), lax.rem(gy + 15, 16)

    loads = [
        pltpu.make_async_copy(src, dst, load_sem.at[n])
        for n, (src, dst) in enumerate(((preact, pv), (cotangent, cv), (source, sv), (kernel, kv)))
    ]
    for copy in loads:
        copy.start()

    a_to, b_to, z_to = [], [], []
    for k in (1, 2, 3):
        a_to.append(spot(lax.rem(y + k * other, 4), lax.rem(x + k * core, 4), core, z))
        b_to.append(spot(lax.rem(y + k * core, 4), lax.rem(x + k * other, 4), core, z))
    for k in range(1, DEPTH):
        z_to.append(spot(y, x, core, lax.rem(z + k, DEPTH)))
    sides = [
        (up_x, gy), (dn_x, gy), (gx, up_y), (gx, dn_y),
        (up_x, up_y), (up_x, dn_y), (dn_x, up_y), (dn_x, dn_y),
    ]
    partner = spot(y, x, other, z)
    everyone = sides + [partner] + a_to + b_to + z_to
    barrier = pltpu.get_barrier_semaphore()
    for device in everyone:
        pl.semaphore_signal(barrier, inc=1, device_id=device, device_id_type=MESH)

    loads[0].wait()
    loads[1].wait()
    for c in range(0, C, 8):
        keep = pv[c : c + 8].astype(F32) > 0
        masked = jnp.where(keep, cv[c : c + 8].astype(F32), 0.0)
        wide[c * 16 : c * 16 + 128, :] = masked.reshape(128, NZ)
    for i in range(WX):
        for j in range(WY):
            slope[i + 1, j + 1] = wide[pl.ds(i * WY + j, C, stride=WX * WY), :].astype(BF16)

    pl.semaphore_wait(barrier, len(everyone))
    ends = [
        (slope.at[2, 1:9], slope.at[0, 1:9]),
        (slope.at[1, 1:9], slope.at[3, 1:9]),
        (slope.at[1:3, 8], slope.at[1:3, 0]),
        (slope.at[1:3, 1], slope.at[1:3, 9]),
        (slope.at[2, 8], slope.at[0, 0]),
        (slope.at[2, 1], slope.at[0, 9]),
        (slope.at[1, 8], slope.at[3, 0]),
        (slope.at[1, 1], slope.at[3, 9]),
    ]
    halos = []
    for n, ((src, dst), device) in enumerate(zip(ends, sides)):
        copy = pltpu.make_async_remote_copy(
            src, dst, halo_send.at[n], halo_recv.at[n], device_id=device, device_id_type=MESH
        )
        copy.start()
        halos.append(copy)

    loads[2].wait()
    for c in range(0, C, 8):
        wide_src[c * 16 : c * 16 + 128, :] = sv[c : c + 8].astype(F32).reshape(128, NZ)
    for i in range(WX):
        for j in range(WY):
            block = wide_src[pl.ds(i * WY + j, C, stride=WX * WY), :]
            for c, shift in enumerate((1, 0, NZ - 1)):
                moved = pltpu.roll(block, shift, 1) if shift else block
                src3[i, j // 2, c * C : (c + 1) * C, (j % 2) * NZ : (j % 2 + 1) * NZ] = moved.astype(BF16)
    loads[3].wait()
    for c in range(3):
        for ab in range(0, 9, 2):
            taps = [kv[3 * n + c].astype(F32) for n in range(ab, min(ab + 2, 9))]
            pair = jnp.concatenate(taps, axis=0) if len(taps) > 1 else taps[0]
            weights[c * C : (c + 1) * C, ab * C : (ab + len(taps)) * C] = pair.T.astype(BF16)

    for copy in halos:
        copy.wait_recv()

    def columns(a, b, i, jp):
        return jnp.concatenate([slope[i + 2 - a, 2 * jp + 2 - b], slope[i + 2 - a, 2 * jp + 3 - b]], axis=1)

    sends = []
    for a in range(3):
        total = None
        for i in range(WX):
            for jp in range(WY // 2):
                left = jnp.concatenate([columns(a, b, i, jp) for b in range(3)], axis=0)
                term = lax.dot_general(left, src3[i, jp], NT, preferred_element_type=F32)
                total = term if total is None else total + term
        prod_lo[a * 192 : (a + 1) * 192, :] = total[:, :128]
        prod_hi[a * 192 : (a + 1) * 192, 0:C] = total[:, 128:]
        for b in range(3):
            base = (a * 3 + b) * C
            lo = [prod_lo[pl.ds(base + odd, 32, stride=2), :] for odd in (0, 1)]
            hi = [prod_hi[pl.ds(base + odd, 32, stride=2), :] for odd in (0, 1)]
            pairs = (
                jnp.concatenate([lo[0][:, :C], lo[1][:, :C]], axis=1),
                jnp.concatenate([lo[0][:, C:], lo[1][:, C:]], axis=1),
                jnp.concatenate([hi[0][:, :C], hi[1][:, :C]], axis=1),
            )
            for c, rows in enumerate(pairs):
                start = 32 * ((a * 3 + b) * 3 + c)
                at = start
                while at < start + 32:
                    q, r = divmod(at, ROWS)
                    count = min(ROWS - r, start + 32 - at)
                    part[(q >> 1) & 1, q >> 3, ((q >> 2) & 1) * 2 + (q & 1), r : r + count, :] = (
                        rows[at - start : at - start + count, :]
                    )
                    at += count
        for n in ((0,), (1,), (2, 3))[a]:
            copy = pltpu.make_async_remote_copy(
                part.at[other, n], core_in.at[n], core_send.at[n], core_recv.at[n],
                device_id=partner, device_id_type=MESH,
            )
            copy.start()
            sends.append(copy)

    def data_gradient(i):
        for jp in range(WY // 2):
            right = jnp.concatenate([columns(a, b, i, jp) for a in range(3) for b in range(3)], axis=0)
            out = jnp.dot(weights[...], right, preferred_element_type=F32)
            for half_at in range(2):
                three = [
                    out[c * C : (c + 1) * C, half_at * NZ : (half_at + 1) * NZ] for c in range(3)
                ]
                whole = pltpu.roll(three[0], NZ - 1, 1) + three[1] + pltpu.roll(three[2], 1, 1)
                wide_out[pl.ds(i * WY + 2 * jp + half_at, C, stride=WX * WY), :] = whole

    data_gradient(0)

    a_me = y * other + x * core
    b_me = x * other + y * core
    for n in range(4):
        sends[n].wait_recv()
        for m in range(4):
            at = (n * other + m * core) * 4 + m * other + n * core
            half[at] = part[core, n, m] + core_in[n, m]
    a_copies = []
    for k in (1, 2, 3):
        copy = pltpu.make_async_remote_copy(
            half.at[pl.ds(lax.rem(a_me + k, 4) * 4, 4)], a_in.at[k - 1], a_send.at[k - 1], a_recv.at[k - 1],
            device_id=a_to[k - 1], device_id_type=MESH,
        )
        copy.start()
        a_copies.append(copy)

    data_gradient(1)

    for copy in a_copies:
        copy.wait_recv()
    for m in range(4):
        quarter[m] = half[a_me * 4 + m] + a_in[0, m] + a_in[1, m] + a_in[2, m]
    b_copies = []
    for k in (1, 2, 3):
        copy = pltpu.make_async_remote_copy(
            quarter.at[lax.rem(b_me + k, 4)], b_in.at[k - 1], b_send.at[k - 1], b_recv.at[k - 1],
            device_id=b_to[k - 1], device_id_type=MESH,
        )
        copy.start()
        b_copies.append(copy)

    for c in range(0, C, 8):
        gs_out[c : c + 8] = wide_out[c * 16 : c * 16 + 128, :].reshape(8, WX, WY, NZ).astype(BF16)

    for copy in b_copies:
        copy.wait_recv()
    last[...] = quarter[b_me] + b_in[0] + b_in[1] + b_in[2]
    lane = lax.broadcasted_iota(jnp.int32, (8, NZ), 1)
    for n in range(DEPTH):
        row, off = divmod(n * OWN, NZ)
        lower = last[row : row + 8, :]
        upper = last[row + 1 : row + 9, :]
        if off:
            lower = jnp.where(lane < NZ - off, pltpu.roll(lower, NZ - off, 1), pltpu.roll(upper, NZ - off, 1))
        z_out[n] = lower
    z_copies = []
    for k in range(1, DEPTH):
        copy = pltpu.make_async_remote_copy(
            z_out.at[lax.rem(z + k, DEPTH)], z_in.at[k - 1], z_send.at[k - 1], z_recv.at[k - 1],
            device_id=z_to[k - 1], device_id_type=MESH,
        )
        copy.start()
        z_copies.append(copy)
    for copy in z_copies:
        copy.wait_recv()
    mine = z_out[z]
    for k in range(DEPTH - 1):
        mine = mine + z_in[k]
    gk_out[...] = mine * (1.0 / math.sqrt(CELLS))

    for copy in halos + sends + a_copies + b_copies + z_copies:
        copy.wait_send()


def on_device(source, preact, cotangent, kernel):
    dma = pltpu.SemaphoreType.DMA
    blocks = (WX + 2, WY + 2, C, NZ)
    grad_source, grad_kernel = pl.pallas_call(
        body,
        out_shape=(
            jax.ShapeDtypeStruct(source.shape, BF16),
            jax.ShapeDtypeStruct((8, NZ), F32),
        ),
        in_specs=[pl.BlockSpec(memory_space=pl.ANY)] * 4,
        out_specs=(pl.BlockSpec(memory_space=pltpu.VMEM), pl.BlockSpec(memory_space=pltpu.VMEM)),
        scratch_shapes=[
            pltpu.VMEM(source.shape, BF16),
            pltpu.VMEM(source.shape, BF16),
            pltpu.VMEM(source.shape, BF16),
            pltpu.VMEM(kernel.shape, BF16),
            pltpu.VMEM((C * WX * WY, NZ), F32),
            pltpu.VMEM((C * WX * WY, NZ), F32),
            pltpu.VMEM((C * WX * WY, NZ), F32),
            pltpu.VMEM(blocks, BF16),
            pltpu.VMEM((WX, WY // 2, 3 * C, 2 * NZ), BF16),
            pltpu.VMEM((3 * C, 9 * C), BF16),
            pltpu.VMEM((9 * C, NZ), F32),
            pltpu.VMEM((9 * C, NZ), F32),
            pltpu.VMEM((2, 4, 4, 32, NZ), F32),
            pltpu.VMEM((4, 4, 32, NZ), F32),
            pltpu.VMEM((16, 32, NZ), F32),
            pltpu.VMEM((3, 4, 32, NZ), F32),
            pltpu.VMEM((4, 32, NZ), F32),
            pltpu.VMEM((3, 32, NZ), F32),
            pltpu.VMEM((32, NZ), F32),
            pltpu.VMEM((8, 8, NZ), F32),
            pltpu.VMEM((7, 8, NZ), F32),
            dma((4,)),
            dma((8,)), dma((8,)), dma((4,)), dma((4,)), dma((3,)), dma((3,)),
            dma((3,)), dma((3,)), dma((7,)), dma((7,)),
        ],
        compiler_params=pltpu.CompilerParams(collective_id=0, has_side_effects=True),
    )(source, preact, cotangent, kernel)
    return grad_source, grad_kernel.reshape(-1)[:OWN]


def solution(mesh):
    placed = (P(None, "gx", "gy", None), P(None, "gx", "gy", None), P(None, "gx", "gy", None), P())
    return jax.shard_map(
        on_device,
        mesh=mesh,
        in_specs=placed,
        out_specs=(P(None, "gx", "gy", None), P(("gx", "gy"))),
        check_vma=False,
    )
```

time: 339 us -> 36.1 us (0.11)
  the two profiles are of different devices: /device:TPU:1 before, /device:TPU:32 now
where the time goes in v1:
time: 36.1 us; the launch traced here: 35.9 us
  Pallas kernels  32.4 us (90%)
  local copies, waits for them, and re-layouts  2.92 us (8%)
  between operations  0.65 us (2%)
    pallas_call x1, Pallas kernels, on_device(): pl.pallas_call(body, out_shape=(jax.ShapeDtypeStruct(source.shape, BF16),...  32.4 us
    unnamed x3, local copies, waits for them, and re-layouts  2.34 us

profile of v1, /device:TPU:32, one launch (start us, length us, event | category | flops | bytes accessed | tf_op | source)
XLA Modules:
  0.0 35.9 jit_solution(12540169012674355696)
XLA Ops:
  0.6 32.4 %shard_map.59 = (bf16[64,2,8,128]{3,2,1,0:T(8,128)(2,1)}, f32[8,128]{1,0:T(8,128)}) custom-call(bf16[64,2,8,128]{3,2,1,0:T(8,128)(2,1)} %source.1, bf16[64,2,8,128]{3,2,1,0:T(8,128)(2,1)} %preact.1, bf16[64,2,8,128]{3,2,1,0:T(8,128)(2,1)} %cotangent.1, bf16[27,64,64]{2,1,0:T(8,128)(2,1)} %kernel.1), custom_call_target="tpu_custom_call" | custom-call | tf_op jit(solution)/shard_map/pallas_call | solution.py:234
  33.0 0.0 copy-start
  33.0 0.7 %copy-done = f32[8,128]{1,0:T(8,128)S(1)} copy-done((f32[8,128]{1,0:T(8,128)S(1)}, f32[8,128]{1,0:T(8,128)}, u32[]{:S(2)}) %copy-start) | copy-done | bytes 4120
  33.7 0.6 %slice.3 = f32[432]{0:T(512)} slice(f32[1024]{0:T(1024)S(1)} %bitcast.1), slice={[0:432]} | slice | bytes 3456 | tf_op jit(solution)/shard_map/slice | solution.py:270
  34.3 1.7 %copy.7 = bf16[64,2,8,128]{3,2,1,0:T(8,128)(2,1)} copy(bf16[64,2,8,128]{3,2,1,0:T(8,128)(2,1)} %get-tuple-element.8) | data formatting | bytes 524288
Async XLA Ops:
  33.0 0.7 %copy-start = (f32[8,128]{1,0:T(8,128)S(1)}, f32[8,128]{1,0:T(8,128)}, u32[]{:S(2)}) copy-start(f32[8,128]{1,0:T(8,128)} %get-tuple-element.5) | copy-start | bytes 12292

commit v2 on v1

--- a/solution.py
+++ b/solution.py
@@ -14,6 +14,10 @@
 DEPTH = 8
 ROWS = 27
 OWN = 432
+PLANE = sorted(
+    ((dy, dx) for dy in range(4) for dx in range(4) if dy or dx),
+    key=lambda d: -min(d[0], 4 - d[0]) - min(d[1], 4 - d[1]),
+)
 CELLS = 32 * 128 * 128
 NT = (((1,), (1,)), ((), ()))
 
@@ -28,8 +32,8 @@
 def body(
     source, preact, cotangent, kernel, gs_out, gk_out,
     pv, cv, sv, kv, wide, wide_src, wide_out, slope, src3, weights, prod_lo, prod_hi,
-    part, core_in, half, a_in, quarter, b_in, last, z_out, z_in,
-    load_sem, halo_send, halo_recv, core_send, core_recv, a_send, a_recv, b_send, b_recv, z_send, z_recv,
+    part, core_in, half, plane_in, last, z_out, z_in,
+    load_sem, halo_send, halo_recv, core_send, core_recv, plane_send, plane_recv, z_send, z_recv,
 ):
     gx, gy = lax.axis_index("gx"), lax.axis_index("gy")
     core, xhi, y = lax.rem(gx, 2), lax.rem(lax.div(gx, 2), 2), lax.div(gx, 4)
@@ -47,10 +51,11 @@
     for copy in loads:
         copy.start()
 
-    a_to, b_to, z_to = [], [], []
-    for k in (1, 2, 3):
-        a_to.append(spot(lax.rem(y + k * other, 4), lax.rem(x + k * core, 4), core, z))
-        b_to.append(spot(lax.rem(y + k * core, 4), lax.rem(x + k * other, 4), core, z))
+    plane_at, plane_to, z_to = [], [], []
+    for dy, dx in PLANE:
+        to_y, to_x = lax.rem(y + dy, 4), lax.rem(x + dx, 4)
+        plane_at.append(to_y * 4 + to_x)
+        plane_to.append(spot(to_y, to_x, core, z))
     for k in range(1, DEPTH):
         z_to.append(spot(y, x, core, lax.rem(z + k, DEPTH)))
     sides = [
@@ -58,7 +63,7 @@
         (up_x, up_y), (up_x, dn_y), (dn_x, up_y), (dn_x, dn_y),
     ]
     partner = spot(y, x, other, z)
-    everyone = sides + [partner] + a_to + b_to + z_to
+    everyone = sides + [partner] + plane_to + z_to
     barrier = pltpu.get_barrier_semaphore()
     for device in everyone:
         pl.semaphore_signal(barrier, inc=1, device_id=device, device_id_type=MESH)
@@ -164,43 +169,28 @@
 
     data_gradient(0)
 
-    a_me = y * other + x * core
-    b_me = x * other + y * core
     for n in range(4):
         sends[n].wait_recv()
         for m in range(4):
-            at = (n * other + m * core) * 4 + m * other + n * core
-            half[at] = part[core, n, m] + core_in[n, m]
-    a_copies = []
-    for k in (1, 2, 3):
+            half[n * 4 + m] = (part[core, n, m] + core_in[n, m]).astype(BF16)
+    plane_copies = []
+    for k, (at, device) in enumerate(zip(plane_at, plane_to)):
         copy = pltpu.make_async_remote_copy(
-            half.at[pl.ds(lax.rem(a_me + k, 4) * 4, 4)], a_in.at[k - 1], a_send.at[k - 1], a_recv.at[k - 1],
-            device_id=a_to[k - 1], device_id_type=MESH,
+            half.at[at], plane_in.at[k], plane_send.at[k], plane_recv.at[k],
+            device_id=device, device_id_type=MESH,
         )
         copy.start()
-        a_copies.append(copy)
+        plane_copies.append(copy)
 
     data_gradient(1)
-
-    for copy in a_copies:
-        copy.wait_recv()
-    for m in range(4):
-        quarter[m] = half[a_me * 4 + m] + a_in[0, m] + a_in[1, m] + a_in[2, m]
-    b_copies = []
-    for k in (1, 2, 3):
-        copy = pltpu.make_async_remote_copy(
-            quarter.at[lax.rem(b_me + k, 4)], b_in.at[k - 1], b_send.at[k - 1], b_recv.at[k - 1],
-            device_id=b_to[k - 1], device_id_type=MESH,
-        )
-        copy.start()
-        b_copies.append(copy)
-
     for c in range(0, C, 8):
         gs_out[c : c + 8] = wide_out[c * 16 : c * 16 + 128, :].reshape(8, WX, WY, NZ).astype(BF16)
 
-    for copy in b_copies:
-        copy.wait_recv()
-    last[...] = quarter[b_me] + b_in[0] + b_in[1] + b_in[2]
+    total = part[core, y, x] + core_in[y, x]
+    for k in reversed(range(len(PLANE))):
+        plane_copies[k].wait_recv()
+        total = total + plane_in[k].astype(F32)
+    last[...] = total
     lane = lax.broadcasted_iota(jnp.int32, (8, NZ), 1)
     for n in range(DEPTH):
         row, off = divmod(n * OWN, NZ)
@@ -224,7 +214,7 @@
         mine = mine + z_in[k]
     gk_out[...] = mine * (1.0 / math.sqrt(CELLS))
 
-    for copy in halos + sends + a_copies + b_copies + z_copies:
+    for copy in halos + sends + plane_copies + z_copies:
         copy.wait_send()
 
 
@@ -234,8 +224,8 @@
     grad_source, grad_kernel = pl.pallas_call(
         body,
         out_shape=(
-            jax.ShapeDtypeStruct(source.shape, BF16),
-            jax.ShapeDtypeStruct((8, NZ), F32),
+            pltpu.VMEM(source.shape, BF16),
+            pltpu.VMEM((8, NZ), F32),
         ),
         in_specs=[pl.BlockSpec(memory_space=pl.ANY)] * 4,
         out_specs=(pl.BlockSpec(memory_space=pltpu.VMEM), pl.BlockSpec(memory_space=pltpu.VMEM)),
@@ -254,16 +244,14 @@
             pltpu.VMEM((9 * C, NZ), F32),
             pltpu.VMEM((2, 4, 4, 32, NZ), F32),
             pltpu.VMEM((4, 4, 32, NZ), F32),
-            pltpu.VMEM((16, 32, NZ), F32),
-            pltpu.VMEM((3, 4, 32, NZ), F32),
-            pltpu.VMEM((4, 32, NZ), F32),
-            pltpu.VMEM((3, 32, NZ), F32),
+            pltpu.VMEM((16, 32, NZ), BF16),
+            pltpu.VMEM((15, 32, NZ), BF16),
             pltpu.VMEM((32, NZ), F32),
             pltpu.VMEM((8, 8, NZ), F32),
             pltpu.VMEM((7, 8, NZ), F32),
             dma((4,)),
-            dma((8,)), dma((8,)), dma((4,)), dma((4,)), dma((3,)), dma((3,)),
-            dma((3,)), dma((3,)), dma((7,)), dma((7,)),
+            dma((8,)), dma((8,)), dma((4,)), dma((4,)), dma((15,)), dma((15,)),
+            dma((7,)), dma((7,)),
         ],
         compiler_params=pltpu.CompilerParams(collective_id=0, has_side_effects=True),
     )(source, preact, cotangent, kernel)

time: 36.1 us -> 31 us (0.86)
  the two profiles are of different devices: /device:TPU:32 before, /device:TPU:1 now
where the time goes in v2:
time: 31 us; the launch traced here: 30.9 us
  Pallas kernels  29 us (94%)
  local copies, waits for them, and re-layouts  1.28 us (4%)
  between operations  0.64 us (2%)
    pallas_call x1, Pallas kernels, on_device(): pl.pallas_call(body, out_shape=(pltpu.VMEM(source.shape, BF16), pltpu.VME...  29 us
    unnamed x1, local copies, waits for them, and re-layouts  0.71 us

profile of v2, /device:TPU:1, one launch (start us, length us, event | category | flops | bytes accessed | tf_op | source)
XLA Modules:
  0.0 30.9 jit_solution(4696014173278763577)
XLA Ops:
  0.6 29.0 %shard_map.59 = (bf16[64,2,8,128]{3,2,1,0:T(8,128)(2,1)S(1)}, f32[8,128]{1,0:T(8,128)S(1)}) custom-call(bf16[64,2,8,128]{3,2,1,0:T(8,128)(2,1)} %source.1, bf16[64,2,8,128]{3,2,1,0:T(8,128)(2,1)} %preact.1, bf16[64,2,8,128]{3,2,1,0:T(8,128)(2,1)} %cotangent.1, bf16[27,64,64]{2,1,0:T(8,128)(2,1)} %kernel.1), custom_call_target="tpu_custom_call" | custom-call | tf_op jit(solution)/shard_map/pallas_call | solution.py:224
  29.6 0.7 %copy.7 = bf16[64,2,8,128]{3,2,1,0:T(8,128)(2,1)} copy(bf16[64,2,8,128]{3,2,1,0:T(8,128)(2,1)S(1)} %get-tuple-element.6) | data formatting | bytes 524288
  30.4 0.6 %slice.3 = f32[432]{0:T(512)} slice(f32[1024]{0:T(1024)S(1)} %bitcast.1), slice={[0:432]} | slice | bytes 3456 | tf_op jit(solution)/shard_map/slice | solution.py:258

commit v3 on v2

--- a/solution.py
+++ b/solution.py
@@ -113,14 +113,13 @@
             pair = jnp.concatenate(taps, axis=0) if len(taps) > 1 else taps[0]
             weights[c * C : (c + 1) * C, ab * C : (ab + len(taps)) * C] = pair.T.astype(BF16)
 
-    for copy in halos:
-        copy.wait_recv()
-
     def columns(a, b, i, jp):
         return jnp.concatenate([slope[i + 2 - a, 2 * jp + 2 - b], slope[i + 2 - a, 2 * jp + 3 - b]], axis=1)
 
     sends = []
-    for a in range(3):
+    for a in (1, 0, 2):
+        for n in ((1, 6, 7), (2, 3), (0, 4, 5))[a]:
+            halos[n].wait_recv()
         total = None
         for i in range(WX):
             for jp in range(WY // 2):
@@ -148,7 +147,7 @@
                         rows[at - start : at - start + count, :]
                     )
                     at += count
-        for n in ((0,), (1,), (2, 3))[a]:
+        for n in ((0, 1), (), (2, 3))[a]:
             copy = pltpu.make_async_remote_copy(
                 part.at[other, n], core_in.at[n], core_send.at[n], core_recv.at[n],
                 device_id=partner, device_id_type=MESH,
@@ -212,7 +211,10 @@
     mine = z_out[z]
     for k in range(DEPTH - 1):
         mine = mine + z_in[k]
-    gk_out[...] = mine * (1.0 / math.sqrt(CELLS))
+    mine = mine * (1.0 / math.sqrt(CELLS))
+    for row in range(0, OWN, NZ):
+        count = min(NZ, OWN - row)
+        gk_out[row : row + count] = mine[row // NZ, :count]
 
     for copy in halos + sends + plane_copies + z_copies:
         copy.wait_send()
@@ -225,7 +227,7 @@
         body,
         out_shape=(
             pltpu.VMEM(source.shape, BF16),
-            pltpu.VMEM((8, NZ), F32),
+            pltpu.VMEM((OWN,), F32),
         ),
         in_specs=[pl.BlockSpec(memory_space=pl.ANY)] * 4,
         out_specs=(pl.BlockSpec(memory_space=pltpu.VMEM), pl.BlockSpec(memory_space=pltpu.VMEM)),
@@ -255,7 +257,7 @@
         ],
         compiler_params=pltpu.CompilerParams(collective_id=0, has_side_effects=True),
     )(source, preact, cotangent, kernel)
-    return grad_source, grad_kernel.reshape(-1)[:OWN]
+    return grad_source, grad_kernel
 
 
 def solution(mesh):

time: 31 us -> 30.4 us (0.981)
  Pallas kernels: 29 us -> 28.4 us
    pallas_call x1, Pallas kernels: 29 us -> 28.4 us  [on_device(): pl.pallas_call(body, out_shape=(pltpu.VMEM(source.shape, BF16), pltpu.VME...]
    slice x1 -> x0, local copies, waits for them, and re-layouts: 0.58 us -> none  [on_device(): return (grad_source, grad_kernel.reshape(-1)[:OWN])]
    unnamed x1 -> x2, local copies, waits for them, and re-layouts: 0.71 us -> 1.28 us
where the time goes in v3:
time: 30.4 us; the launch traced here: 30.3 us
  Pallas kernels  28.4 us (93%)
  local copies, waits for them, and re-layouts  1.28 us (4%)
  between operations  0.64 us (2%)
    pallas_call x1, Pallas kernels, on_device(): pl.pallas_call(body, out_shape=(pltpu.VMEM(source.shape, BF16), pltpu.VME...  28.4 us
    unnamed x2, local copies, waits for them, and re-layouts  1.28 us

profile of v3, /device:TPU:1, one launch (start us, length us, event | category | flops | bytes accessed | tf_op | source)
XLA Modules:
  0.0 30.3 jit_solution(10438350212188033809)
XLA Ops:
  0.6 28.4 %shard_map.59 = (bf16[64,2,8,128]{3,2,1,0:T(8,128)(2,1)S(1)}, f32[432]{0:T(512)S(1)}) custom-call(bf16[64,2,8,128]{3,2,1,0:T(8,128)(2,1)} %source.1, bf16[64,2,8,128]{3,2,1,0:T(8,128)(2,1)} %preact.1, bf16[64,2,8,128]{3,2,1,0:T(8,128)(2,1)} %cotangent.1, bf16[27,64,64]{2,1,0:T(8,128)(2,1)} %kernel.1), custom_call_target="tpu_custom_call" | custom-call | tf_op jit(solution)/shard_map/pallas_call | solution.py:226
  29.0 0.7 %copy.8 = bf16[64,2,8,128]{3,2,1,0:T(8,128)(2,1)} copy(bf16[64,2,8,128]{3,2,1,0:T(8,128)(2,1)S(1)} %get-tuple-element.2) | data formatting | bytes 524288
  29.7 0.6 %copy.9 = f32[432]{0:T(512)} copy(f32[432]{0:T(512)S(1)} %get-tuple-element.3) | data formatting | bytes 3456

commit v4 on v3

--- a/solution.py
+++ b/solution.py
@@ -15,7 +15,7 @@
 ROWS = 27
 OWN = 432
 PLANE = sorted(
-    ((dy, dx) for dy in range(4) for dx in range(4) if dy or dx),
+    ((dy, dx, dc) for dy in range(4) for dx in range(4) for dc in range(2) if dy or dx or dc),
     key=lambda d: -min(d[0], 4 - d[0]) - min(d[1], 4 - d[1]),
 )
 CELLS = 32 * 128 * 128
@@ -32,8 +32,8 @@
 def body(
     source, preact, cotangent, kernel, gs_out, gk_out,
     pv, cv, sv, kv, wide, wide_src, wide_out, slope, src3, weights, prod_lo, prod_hi,
-    part, core_in, half, plane_in, last, z_out, z_in,
-    load_sem, halo_send, halo_recv, core_send, core_recv, plane_send, plane_recv, z_send, z_recv,
+    part, half, plane_in, last, z_out, z_in,
+    load_sem, halo_send, halo_recv, plane_send, plane_recv, z_send, z_recv,
 ):
     gx, gy = lax.axis_index("gx"), lax.axis_index("gy")
     core, xhi, y = lax.rem(gx, 2), lax.rem(lax.div(gx, 2), 2), lax.div(gx, 4)
@@ -52,18 +52,18 @@
         copy.start()
 
     plane_at, plane_to, z_to = [], [], []
-    for dy, dx in PLANE:
+    for dy, dx, dc in PLANE:
+        to_core = other if dc else core
         to_y, to_x = lax.rem(y + dy, 4), lax.rem(x + dx, 4)
-        plane_at.append(to_y * 4 + to_x)
-        plane_to.append(spot(to_y, to_x, core, z))
+        plane_at.append(to_core * 16 + to_y * 4 + to_x)
+        plane_to.append(spot(to_y, to_x, to_core, z))
     for k in range(1, DEPTH):
         z_to.append(spot(y, x, core, lax.rem(z + k, DEPTH)))
     sides = [
         (up_x, gy), (dn_x, gy), (gx, up_y), (gx, dn_y),
         (up_x, up_y), (up_x, dn_y), (dn_x, up_y), (dn_x, dn_y),
     ]
-    partner = spot(y, x, other, z)
-    everyone = sides + [partner] + plane_to + z_to
+    everyone = sides + plane_to + z_to
     barrier = pltpu.get_barrier_semaphore()
     for device in everyone:
         pl.semaphore_signal(barrier, inc=1, device_id=device, device_id_type=MESH)
@@ -116,7 +116,6 @@
     def columns(a, b, i, jp):
         return jnp.concatenate([slope[i + 2 - a, 2 * jp + 2 - b], slope[i + 2 - a, 2 * jp + 3 - b]], axis=1)
 
-    sends = []
     for a in (1, 0, 2):
         for n in ((1, 6, 7), (2, 3), (0, 4, 5))[a]:
             halos[n].wait_recv()
@@ -147,13 +146,6 @@
                         rows[at - start : at - start + count, :]
                     )
                     at += count
-        for n in ((0, 1), (), (2, 3))[a]:
-            copy = pltpu.make_async_remote_copy(
-                part.at[other, n], core_in.at[n], core_send.at[n], core_recv.at[n],
-                device_id=partner, device_id_type=MESH,
-            )
-            copy.start()
-            sends.append(copy)
 
     def data_gradient(i):
         for jp in range(WY // 2):
@@ -166,12 +158,10 @@
                 whole = pltpu.roll(three[0], NZ - 1, 1) + three[1] + pltpu.roll(three[2], 1, 1)
                 wide_out[pl.ds(i * WY + 2 * jp + half_at, C, stride=WX * WY), :] = whole
 
-    data_gradient(0)
-
-    for n in range(4):
-        sends[n].wait_recv()
-        for m in range(4):
-            half[n * 4 + m] = (part[core, n, m] + core_in[n, m]).astype(BF16)
+    for c in range(2):
+        for n in range(4):
+            for m in range(4):
+                half[c * 16 + n * 4 + m] = part[c, n, m].astype(BF16)
     plane_copies = []
     for k, (at, device) in enumerate(zip(plane_at, plane_to)):
         copy = pltpu.make_async_remote_copy(
@@ -181,11 +171,12 @@
         copy.start()
         plane_copies.append(copy)
 
+    data_gradient(0)
     data_gradient(1)
     for c in range(0, C, 8):
         gs_out[c : c + 8] = wide_out[c * 16 : c * 16 + 128, :].reshape(8, WX, WY, NZ).astype(BF16)
 
-    total = part[core, y, x] + core_in[y, x]
+    total = part[core, y, x]
     for k in reversed(range(len(PLANE))):
         plane_copies[k].wait_recv()
         total = total + plane_in[k].astype(F32)
@@ -216,7 +207,7 @@
         count = min(NZ, OWN - row)
         gk_out[row : row + count] = mine[row // NZ, :count]
 
-    for copy in halos + sends + plane_copies + z_copies:
+    for copy in halos + plane_copies + z_copies:
         copy.wait_send()
 
 
@@ -245,14 +236,13 @@
             pltpu.VMEM((9 * C, NZ), F32),
             pltpu.VMEM((9 * C, NZ), F32),
             pltpu.VMEM((2, 4, 4, 32, NZ), F32),
-            pltpu.VMEM((4, 4, 32, NZ), F32),
-            pltpu.VMEM((16, 32, NZ), BF16),
-            pltpu.VMEM((15, 32, NZ), BF16),
+            pltpu.VMEM((32, 32, NZ), BF16),
+            pltpu.VMEM((31, 32, NZ), BF16),
             pltpu.VMEM((32, NZ), F32),
             pltpu.VMEM((8, 8, NZ), F32),
             pltpu.VMEM((7, 8, NZ), F32),
             dma((4,)),
-            dma((8,)), dma((8,)), dma((4,)), dma((4,)), dma((15,)), dma((15,)),
+            dma((8,)), dma((8,)), dma((31,)), dma((31,)),
             dma((7,)), dma((7,)),
         ],
         compiler_params=pltpu.CompilerParams(collective_id=0, has_side_effects=True),

time: 30.4 us -> 30.6 us (level)
  no operation moved by 1% of the time
where the time goes in v4:
time: 30.6 us; the launch traced here: 30.5 us
  Pallas kernels  28.6 us (93%)
  local copies, waits for them, and re-layouts  1.28 us (4%)
  between operations  0.64 us (2%)
    pallas_call x1, Pallas kernels, on_device(): pl.pallas_call(body, out_shape=(pltpu.VMEM(source.shape, BF16), pltpu.VME...  28.6 us
    unnamed x2, local copies, waits for them, and re-layouts  1.28 us

profile of v4, /device:TPU:1, one launch (start us, length us, event | category | flops | bytes accessed | tf_op | source)
XLA Modules:
  0.0 30.5 jit_solution(4038113495897421144)
XLA Ops:
  0.6 28.6 %shard_map.59 = (bf16[64,2,8,128]{3,2,1,0:T(8,128)(2,1)S(1)}, f32[432]{0:T(512)S(1)}) custom-call(bf16[64,2,8,128]{3,2,1,0:T(8,128)(2,1)} %source.1, bf16[64,2,8,128]{3,2,1,0:T(8,128)(2,1)} %preact.1, bf16[64,2,8,128]{3,2,1,0:T(8,128)(2,1)} %cotangent.1, bf16[27,64,64]{2,1,0:T(8,128)(2,1)} %kernel.1), custom_call_target="tpu_custom_call" | custom-call | tf_op jit(solution)/shard_map/pallas_call | solution.py:217
  29.2 0.7 %copy.8 = bf16[64,2,8,128]{3,2,1,0:T(8,128)(2,1)} copy(bf16[64,2,8,128]{3,2,1,0:T(8,128)(2,1)S(1)} %get-tuple-element.2) | data formatting | bytes 524288
  30.0 0.6 %copy.9 = f32[432]{0:T(512)} copy(f32[432]{0:T(512)S(1)} %get-tuple-element.3) | data formatting | bytes 3456
